TPU v7x, 256 devices: a whole 4x4x8 slice. The times are simulated.
256 devices in a mesh: dp: 32 (over z_lo, y, x), tensor: 8 (over z_hi, core).
Axes of the slice: x: 4, y: 4, z: 8 (z_hi: 4, z_lo: 2; z = z_hi * 2 + z_lo), core: 2. Of those that a mesh axis runs over, the one named last changes fastest.
Arguments:
- rollout_rows: bfloat16 [16384, 4608], P(('dp', 'tensor')), may hold values from -6 to 6
- pack_dest: int32 [16384], P(('dp', 'tensor')), may hold values from 0 to 16383, as said below
- lengths: int32 [17], replicated, may hold values from 128 to 1536, as said below
- pattern: int32 [128, 128], P('dp'), may hold values from 0 to 1, as said below
- norm_gain: float32 [4608], replicated, may hold values from 0.1 to 1.9
- w_query: bfloat16 [4608, 2048], P(None, 'tensor'), may hold values from -0.1875 to 0.1875
- w_key: bfloat16 [4608, 1024], P(None, 'tensor'), may hold values from -0.1875 to 0.1875
- w_value: bfloat16 [4608, 1024], P(None, 'tensor'), may hold values from -0.09375 to 0.09375
- w_out: bfloat16 [2048, 4608], P('tensor'), may hold values from -0.125 to 0.125
- post_gain: float32 [4608], replicated, may hold values from 0.1 to 1.9
Outputs:
- layer_out: bfloat16 [16384, 4608], P(('dp', 'tensor'))
Inputs may be any that keep to these rules, and one draw needn't show every extreme that they name: `pack_dest`: a permutation of the pack rows; a rollout row goes to a pack row of the same tensor index, and the 64 rollout rows of one device go to each dp index exactly 2 at a time. `lengths`: all multiples of 128, summing to 16384; the prompt is shorter than 512. pattern[q, q] = 1; pattern[q, k] = 1 only where k <= q and key block k lies in the first 512 pack rows or in a dp shard at most 3 before query block q's shard.
All inputs are finite; a program needn't handle non-finite values.
Results may differ from a plain program's by a relative error of at most 0.017.
Values may be sent and summed in bfloat16 or wider, within the bound.
No kernel may reach another device: no remote copies, remote signals or barrier semaphores. Data moves between devices by JAX's collectives and lax.ppermute only.
A program may use at most 128 MiB of HBM per device.

v0:
```python
import jax
import jax.numpy as jnp
from jax import lax
from jax.sharding import PartitionSpec as P

HD = 128
BLK = 128


SOFT_CAP = 50.0
QUERY_SCALE = 1.0 / 12.0
ROPE_BASE = 10000.0
EPSILON = 1e-06


def positions(row_ids, lengths):
    bounds = jnp.cumsum(lengths)
    prompt = lengths[0]
    passed = (row_ids[:, None] >= bounds[None, :]).astype(jnp.int32)
    offset_start = jnp.sum(passed * lengths[None, :], axis=1)
    return jnp.where(row_ids < prompt, row_ids, prompt + row_ids - offset_start)


def rotate(values, angle_pos):
    half_width = values.shape[-1] // 2
    inverse_freq = jnp.power(
        ROPE_BASE, -(jnp.arange(half_width, dtype=jnp.float32) * 2.0) / values.shape[-1]
    )
    angles = angle_pos[:, None] * inverse_freq[None, :]
    cosine = jnp.cos(angles)[:, None, :]
    sine_part = jnp.sin(angles)[:, None, :]
    front_half = values[..., :half_width]
    back_half = values[..., half_width:]
    return jnp.concatenate(
        [front_half * cosine - back_half * sine_part, back_half * cosine + front_half * sine_part],
        axis=-1,
    )


def rms_scale(values, gain):
    return values * lax.rsqrt(jnp.mean(values * values, axis=-1, keepdims=True) + EPSILON) * gain


def attend(running, queries, key_value, pats, q_start, low_block, high_block):
    query_count = queries.shape[0]
    head_count = queries.shape[1]
    head_width = queries.shape[3]
    block_count = key_value.shape[0] // BLK
    key_blocks = key_value.reshape(block_count, BLK, 2, head_count, head_width)
    q_ids = q_start + jnp.arange(query_count, dtype=jnp.int32)

    def step(block_index, current):
        column = lax.dynamic_index_in_dim(
            pats, jnp.clip(block_index, 0, pats.shape[1] - 1), 1, keepdims=False
        )
        active = (block_index >= low_block) & (block_index < high_block) & jnp.any(column == 1)

        def compute(inner):
            weighted, totals = inner
            block_pair = lax.dynamic_index_in_dim(key_blocks, block_index, 0, keepdims=False)
            scores = (
                jnp.einsum(
                    "qhgd,khd->hgqk", queries, block_pair[:, 0], preferred_element_type=jnp.float32
                )
                * QUERY_SCALE
            )
            capped = SOFT_CAP * jnp.tanh(scores / SOFT_CAP)
            k_ids = block_index * BLK + jnp.arange(BLK, dtype=jnp.int32)
            allowed = (jnp.repeat(column, BLK) == 1)[:, None] & (k_ids[None, :] <= q_ids[:, None])
            weights = jnp.where(allowed, jnp.exp(capped), jnp.float32(0.0))
            rounded = weights.astype(jnp.bfloat16)
            weighted = weighted + jnp.einsum(
                "hgqk,khd->hgqd", rounded, block_pair[:, 1], preferred_element_type=jnp.float32
            )
            totals = totals + jnp.sum(weights, axis=-1)
            return (weighted, totals)

        return lax.cond(active, compute, lambda inner: inner, current)

    return lax.fori_loop(0, block_count, step, running)


def body(
    rollout_rows, pack_dest, lengths, pattern, norm_gain, w_query, w_key, w_value, w_out, post_gain
):
    tok_count = rollout_rows.shape[0]
    data_count = lax.axis_size("dp")
    tens_count = lax.axis_size("tensor")
    shard_len = tok_count * tens_count
    per_peer = tok_count // data_count
    target_dev = pack_dest // shard_len
    target_slot = pack_dest % tok_count
    order_ids = jnp.arange(tok_count, dtype=jnp.int32)
    before = (target_dev[:, None] == target_dev[None, :]) & (
        order_ids[None, :] < order_ids[:, None]
    )
    bucket_rank = jnp.sum(before.astype(jnp.int32), axis=1)
    send_pos = target_dev * per_peer + bucket_rank
    placer = order_ids[:, None] == send_pos[None, :]
    send_rows = jnp.dot(
        placer.astype(jnp.bfloat16), rollout_rows, preferred_element_type=jnp.float32
    ).astype(jnp.bfloat16)
    send_slots = jnp.sum(jnp.where(placer, target_slot[None, :], 0), axis=1)
    got_rows, got_slots = (
        lax.all_to_all(
            send_rows.reshape(data_count, per_peer, -1),
            "dp",
            split_axis=0,
            concat_axis=0,
            tiled=True,
        ),
        lax.all_to_all(
            send_slots.reshape(data_count, per_peer), "dp", split_axis=0, concat_axis=0, tiled=True
        ),
    )
    arrange = order_ids[:, None] == got_slots.reshape(tok_count)[None, :]
    packed = jnp.dot(
        arrange.astype(jnp.bfloat16),
        got_rows.reshape(tok_count, -1),
        preferred_element_type=jnp.float32,
    ).astype(jnp.bfloat16)
    normed = rms_scale(packed.astype(jnp.float32), norm_gain).astype(jnp.bfloat16)
    data_index = lax.axis_index("dp")
    base_row = data_index * shard_len
    query_cols = w_query.shape[1]
    pair_cols = w_key.shape[1]
    kv_heads = pair_cols // HD
    group_size = query_cols // HD // kv_heads
    portion = lax.all_gather(normed, "tensor", axis=0, tiled=True)
    row_ids = base_row + jnp.arange(portion.shape[0], dtype=jnp.int32)
    angle_pos = positions(row_ids, lengths).astype(jnp.float32)
    query_part = jnp.dot(portion, w_query, preferred_element_type=jnp.float32)
    key_part = jnp.dot(portion, w_key, preferred_element_type=jnp.float32)
    value_part = jnp.dot(portion, w_value, preferred_element_type=jnp.float32)
    query_part = rotate(query_part.reshape(-1, query_cols // HD, HD), angle_pos).reshape(
        -1, query_cols
    )
    key_part = rotate(key_part.reshape(-1, kv_heads, HD), angle_pos).reshape(-1, pair_cols)
    projected = jnp.concatenate([query_part, key_part, value_part], axis=1).astype(jnp.bfloat16)
    queries = projected[:, :query_cols].reshape(shard_len, kv_heads, group_size, HD)
    key_value = projected[:, query_cols:]
    block_total = pattern.shape[1]
    start_state = (
        jnp.zeros((kv_heads, group_size, shard_len, HD), jnp.float32),
        jnp.zeros((kv_heads, group_size, shard_len), jnp.float32),
    )
    weighted, totals = attend(
        start_state,
        queries,
        lax.all_gather(key_value, "dp", axis=0, tiled=True),
        pattern,
        base_row,
        0,
        block_total,
    )
    attended = weighted / totals[..., None]
    heads_out = (
        jnp.transpose(attended, (2, 0, 1, 3)).reshape(shard_len, query_cols).astype(jnp.bfloat16)
    )
    summed = lax.psum_scatter(
        jnp.dot(heads_out, w_out, preferred_element_type=jnp.float32).astype(jnp.bfloat16),
        "tensor",
        scatter_dimension=0,
        tiled=True,
    ).astype(jnp.float32)
    result = packed.astype(jnp.float32) + rms_scale(summed, post_gain)
    return result.astype(jnp.bfloat16)


def solution(mesh):
    placed = (
        P(("dp", "tensor"), None),
        P(("dp", "tensor")),
        P(),
        P("dp", None),
        P(),
        P(None, "tensor"),
        P(None, "tensor"),
        P(None, "tensor"),
        P("tensor", None),
        P(),
    )
    return jax.shard_map(
        body, mesh=mesh, in_specs=placed, out_specs=P(("dp", "tensor"), None), check_vma=False
    )
```

profile of v0, /device:TPU:40, one launch (start us, length us, event | category | flops | bytes accessed | tf_op | source)
XLA Modules:
  0.0 566.0 jit_solution(9726202630693829458)
XLA Ops:
  6.5 0.8 and_select_fusion
  7.7 0.7 all_to_all.9
  8.4 8.4 %all-to-all-start = ((s32[32,1,2]{2,1,0:T(1,128)}), s32[32,1,2]{2,1,0:T(1,128)S(1)}, u32[]{:S(2)}, u32[]{:S(2)}) async-start(s32[32,1,2]{2,1,0:T(1,128)} %bitcast.12), calls=%async_computation | async-start | bytes 32768 | tf_op jit(solution)/shard_map/all_to_all | solution.py:112
  16.8 1.4 convolution_convert_fusion.2
  18.2 1.0 reshape.231
  19.2 3.8 all-to-all-done
  23.0 6.0 %all-to-all-start.1 = ((bf16[32,2,4608]{2,1,0:T(2,128)(2,1)}), bf16[32,2,4608]{2,1,0:T(2,128)(2,1)S(1)}, u32[]{:S(2)}, u32[]{:S(2)}) async-start(bf16[32,2,4608]{2,1,0:T(2,128)(2,1)} %reshape.231), calls=%async_computation.1 | async-start | bytes 1179648 | tf_op jit(solution)/shard_map/all_to_all | solution.py:105
  29.6 0.7 reduce.5
  30.4 7.9 %all-to-all-done.1 = bf16[32,2,4608]{2,1,0:T(2,128)(2,1)S(1)} async-done(((bf16[32,2,4608]{2,1,0:T(2,128)(2,1)}), bf16[32,2,4608]{2,1,0:T(2,128)(2,1)S(1)}, u32[]{:S(2)}, u32[]{:S(2)}) %all-to-all-start.1) | async-done | bytes 589856 | tf_op jit(solution)/shard_map/all_to_all | solution.py:105
  38.9 1.0 copy-done.2
  39.9 1.0 multiply_convert_fusion
  41.0 0.7 copy.34
  41.7 0.7 reduce-window.8
  43.1 0.7 select_reduce_fusion
  43.8 54.3 %all-gather.3.cloned.1.call-done = bf16[512,4608]{1,0:T(8,128)(2,1)} async-done(((bf16[64,4608]{1,0:T(8,128)(2,1)}), bf16[512,4608]{1,0:T(8,128)(2,1)}) %all-gather.3.cloned.1.call-update) | async-done | bytes 4718608 | tf_op jit(solution)/shard_map/all_gather | solution.py:129
  98.1 4.2 convolution_bitcast_fusion.1
  102.9 1.7 convolution_convert_fusion.3
  104.6 0.7 pad_maximum_fusion
  105.7 1.8 multiply_cosine_fusion
  107.5 4.5 fusion.30
  112.1 0.7 fusion.29
  113.0 1.1 copy.42
  114.2 1.2 subtract_convert_fusion
  115.5 152.7 %all-gather.5.cloned.1.call-done = bf16[16384,256]{0,1:T(8,128)(2,1)} async-done(((bf16[512,256]{0,1:T(8,128)(2,1)}), bf16[16384,256]{0,1:T(8,128)(2,1)}) %all-gather.5.cloned.1.call-update) | async-done | bytes 8388624 | tf_op jit(solution)/shard_map/all_gather | solution.py:150
  268.2 9.2 %copy.43 = bf16[32,8,128,128]{3,2,1,0:T(8,128)(2,1)} copy(bf16[32,8,128,128]{3,1,2,0:T(8,128)(2,1)} %bitcast.70) | data formatting | bytes 16777216
  277.4 13.1 %copy.38 = bf16[128,128,2,1,128]{4,1,2,3,0:T(8,128)(2,1)} copy(bf16[128,128,2,1,128]{1,0,4,2,3:T(8,128)(2,1)} %bitcast.69) | data formatting | bytes 16777216
  290.5 186.8 %while.16 = (s32[]{:T(128)}, f32[1,2,512,128]{3,2,1,0:T(8,128)S(1)}, f32[1,2,512]{2,1,0:T(2,128)S(1)}, s32[4,128]{0,1:T(8,128)S(1)}, bf16[128,128,2,1,128]{4,1,2...) while((s32[]{:T(128)}, ...), condition=%wide.region_10.11_spmd.clone, body=%wide.region_5.10_spmd.clone.sunk | while | flops 68027032 | bytes 2189677 | solution.py:80
  291.8 1.7 conditional.3
  291.8 0.8 dynamic-slice_bitcast_fusion
  293.5 0.6 compare_reduce_fusion.2
  296.2 0.6 compare_reduce_fusion.2
  297.6 0.6 compare_reduce_fusion.2
  300.2 0.6 compare_reduce_fusion.2
  302.9 0.6 compare_reduce_fusion.2
  304.3 0.6 compare_reduce_fusion.2
  306.9 0.6 compare_reduce_fusion.2
  308.3 0.6 compare_reduce_fusion.2
  310.9 0.6 compare_reduce_fusion.2
  313.6 0.6 compare_reduce_fusion.2
  315.0 0.6 compare_reduce_fusion.2
  317.6 0.6 compare_reduce_fusion.2
  319.0 0.6 compare_reduce_fusion.2
  321.7 0.6 compare_reduce_fusion.2
  323.0 0.6 compare_reduce_fusion.2
  395.3 1.7 conditional.3
  395.3 0.8 dynamic-slice_bitcast_fusion
  398.3 1.7 conditional.3
  398.3 0.8 dynamic-slice_bitcast_fusion
  401.4 1.7 conditional.3
  401.4 0.8 dynamic-slice_bitcast_fusion
  404.4 1.7 conditional.3
  404.5 0.8 dynamic-slice_bitcast_fusion
  407.5 1.7 conditional.3
  407.5 0.8 dynamic-slice_bitcast_fusion
  410.5 1.7 conditional.3
  410.6 0.8 dynamic-slice_bitcast_fusion
  413.6 1.7 conditional.3
  413.6 0.8 dynamic-slice_bitcast_fusion
  416.7 1.7 conditional.3
  416.7 0.8 dynamic-slice_bitcast_fusion
  477.6 3.5 convolution_convert_fusion
  481.2 74.8 %reduce-scatter.2.cloned.1.call-done = bf16[64,4608]{1,0:T(8,128)(2,1)} async-done(((bf16[512,4608]{1,0:T(8,128)(2,1)}), bf16[64,4608]{1,0:T(8,128)(2,1)}) %reduce-scatter.2.cloned.1.call-update) | async-done | bytes 589840 | tf_op jit(solution)/shard_map/reduce_scatter | solution.py:160
  556.0 1.3 fusion.12
  557.3 2.1 fusion.15
  (477 shorter events, 85.7 us)
Async XLA Ops:
  6.5 471.1 %copy-start = (bf16[256,4608]{1,0:T(8,128)(2,1)S(1)}, bf16[256,4608]{1,0:T(8,128)(2,1)}, u32[]{:S(2)}) copy-start(bf16[256,4608]{1,0:T(8,128)(2,1)} %param.22) | copy-start | bytes 7077892
  8.4 14.6 %all-to-all-start = ((s32[32,1,2]{2,1,0:T(1,128)}), s32[32,1,2]{2,1,0:T(1,128)S(1)}, u32[]{:S(2)}, u32[]{:S(2)}) async-start(s32[32,1,2]{2,1,0:T(1,128)} %bitcast.12), calls=%async_computation | async-start | bytes 32768 | tf_op jit(solution)/shard_map/all_to_all | solution.py:112
  23.0 15.3 %all-to-all-start.1 = ((bf16[32,2,4608]{2,1,0:T(2,128)(2,1)}), bf16[32,2,4608]{2,1,0:T(2,128)(2,1)S(1)}, u32[]{:S(2)}, u32[]{:S(2)}) async-start(bf16[32,2,4608]{2,1,0:T(2,128)(2,1)} %reshape.231), calls=%async_computation.1 | async-start | bytes 1179648 | tf_op jit(solution)/shard_map/all_to_all | solution.py:105
  29.0 69.1 %all-gather.3.cloned.1.call-start = ((), (), s32[]{:S(2)}) async-start(), calls=%async_computation.3 | async-start | bytes 5308416 | tf_op jit(solution)/shard_map/all_gather | solution.py:129
  38.5 1.4 copy-start.6
  38.9 1.0 copy-start.2
  39.9 1.1 copy-start.7
  39.9 58.2 %copy-start.4 = (bf16[4608,128]{1,0:T(8,128)(2,1)S(1)}, bf16[4608,128]{1,0:T(8,128)(2,1)}, u32[]{:S(2)}) copy-start(bf16[4608,128]{1,0:T(8,128)(2,1)} %param.20) | copy-start | bytes 3538948
  40.9 227.2 %all-gather.5.cloned.1.call-start = ((), (), s32[]{:S(2)}) async-start(), calls=%async_computation.4 | async-start | bytes 8650752 | tf_op jit(solution)/shard_map/all_gather | solution.py:150
  98.1 4.8 copy-start.1
  98.1 4.8 copy-start.5
  102.9 2.7 copy-start.8
  105.4 450.6 %reduce-scatter.2.cloned.1.call-start = ((), (), s32[]{:S(2)}) async-start(), calls=%async_computation.5 | async-start | bytes 5308416 | tf_op jit(solution)/shard_map/reduce_scatter | solution.py:160
  481.1 76.2 %copy-start.3 = (f32[64,4608]{1,0:T(8,128)S(1)}, f32[64,4608]{1,0:T(8,128)}, u32[]{:S(2)}) copy-start(f32[64,4608]{1,0:T(8,128)} %copy-done.2) | copy-start | bytes 3538948
Sparse Core Ops, SparseCore 0:
  41.1 57.0 all-gather.2
  105.5 162.6 all-gather.4
  481.3 74.6 reduce-scatter.1
where the time goes:
time: 570 us; the launch traced here: 566 us
  waiting for transfers between devices  293 us (51%)
  other arithmetic  96.1 us (17%)
  loops' own time  89.4 us (16%)
  local copies, waits for them, and re-layouts  37.6 us (7%)
  matrix products  21.2 us (4%)
  starting transfers between devices  14.8 us (3%)
  between operations  13.4 us (2%)
    all_gather x1, waiting for transfers between devices, body(): lax.all_gather(key_value, 'dp', axis=0, tiled=True)  153 us
    another operation x1, loops' own time, attend(): return lax.fori_loop(0, block_count, step, running)  87.4 us
    reduce_or x128, other arithmetic, step(): jnp.any(column == 1)  82.1 us
    reduce_scatter x1, waiting for transfers between devices, body(): lax.psum_scatter(jnp.dot(heads_out, w_out, preferred_element_type=jnp.flo...  74.8 us
    all_gather x1, waiting for transfers between devices, body(): portion = lax.all_gather(normed, 'tensor', axis=0, tiled=True)  54.3 us
    unnamed x23, local copies, waits for them, and re-layouts  24.7 us
  transfers between devices with their start and end apart: 5, of which 5 were waited for; matrix products, arithmetic and copies ran while one was open for 3% of the time, Pallas kernels for 0%

commit v1 on v0

v1 whole, which is shorter than its diff:
```python
import functools
import math

import jax
import jax.numpy as jnp
from jax import lax
from jax.experimental import pallas as pl
from jax.experimental.pallas import tpu as pltpu
from jax.sharding import PartitionSpec as P

HD = 128
BLK = 128
D = 4608
SHARD = 512
SLOTS = 64
PLANES = 4
RING = 16

SOFT_CAP = 50.0
QUERY_SCALE = 1.0 / 12.0
ROPE_BASE = 10000.0
EPSILON = 1e-06

NEXT = [(t, (t + 2) % 8) for t in range(8)]
PREV = [(t, (t + 6) % 8) for t in range(8)]
FAR = [(t, (t + 4) % 8) for t in range(8)]
SIB = [(t, t ^ 1) for t in range(8)]
VMEM_BYTES = 56 << 20


def positions(row_ids, lengths):
    bounds = jnp.cumsum(lengths)
    prompt = lengths[0]
    passed = (row_ids[:, None] >= bounds[None, :]).astype(jnp.int32)
    offset_start = jnp.sum(passed * lengths[None, :], axis=1)
    return jnp.where(row_ids < prompt, row_ids, prompt + row_ids - offset_start)


def rope_tables(row_ids, lengths):
    angle_pos = positions(row_ids, lengths).astype(jnp.float32)
    half = HD // 2
    inverse_freq = jnp.power(ROPE_BASE, -(jnp.arange(half, dtype=jnp.float32) * 2.0) / HD)
    angles = angle_pos[:, None] * inverse_freq[None, :]
    cosine = jnp.cos(angles)
    sine = jnp.sin(angles)
    return jnp.concatenate([cosine, cosine], 1), jnp.concatenate([-sine, sine], 1)


def rms_scale(values, gain):
    return values * lax.rsqrt(jnp.mean(values * values, axis=-1, keepdims=True) + EPSILON) * gain


def to(values, pairs):
    return lax.ppermute(values, "tensor", pairs)


def qkv_kernel(count, *refs):
    xs = refs[:count]
    wq, wk, wv, cos, sin, q_out, kv_out, acc = refs[count:]
    step = pl.program_id(0)

    @pl.when(step == 0)
    def _():
        acc[...] = jnp.zeros_like(acc)

    x = jnp.concatenate([r[...] for r in xs], axis=0)
    acc[:, :256] += jnp.dot(x, wq[...], preferred_element_type=jnp.float32)
    acc[:, 256:384] += jnp.dot(x, wk[...], preferred_element_type=jnp.float32)
    acc[:, 384:] += jnp.dot(x, wv[...], preferred_element_type=jnp.float32)

    @pl.when(step == pl.num_programs(0) - 1)
    def _():
        c = cos[...]
        s = sin[...]

        def turn(v):
            return (v * c + pltpu.roll(v, HD // 2, 1) * s).astype(jnp.bfloat16)

        q_out[0] = turn(acc[:, :128])
        q_out[1] = turn(acc[:, 128:256])
        kv_out[:, :128] = turn(acc[:, 256:384])
        kv_out[:, 128:] = acc[:, 384:].astype(jnp.bfloat16)


def project(pieces, w_query, w_key, w_value, cos, sin):
    rows = sum(p.shape[0] for p in pieces)
    tile = 512
    in_specs = [pl.BlockSpec((p.shape[0], tile), lambda k: (0, k)) for p in pieces]
    in_specs += [pl.BlockSpec((tile, w.shape[1]), lambda k: (k, 0)) for w in (w_query, w_key, w_value)]
    in_specs += [pl.BlockSpec((rows, HD), lambda k: (0, 0))] * 2
    return pl.pallas_call(
        functools.partial(qkv_kernel, len(pieces)),
        grid=(D // tile,),
        in_specs=in_specs,
        out_specs=[
            pl.BlockSpec((2, rows, HD), lambda k: (0, 0, 0)),
            pl.BlockSpec((rows, 2 * HD), lambda k: (0, 0)),
        ],
        out_shape=[
            jax.ShapeDtypeStruct((2, rows, HD), jnp.bfloat16),
            jax.ShapeDtypeStruct((rows, 2 * HD), jnp.bfloat16),
        ],
        scratch_shapes=[pltpu.VMEM((rows, 512), jnp.float32)],
        compiler_params=pltpu.CompilerParams(vmem_limit_bytes=VMEM_BYTES),
        name="project",
    )(*pieces, w_query, w_key, w_value, cos, sin)


def attend_kernel(tab, core, q_a, q_c, *refs):
    kvs = refs[:8]
    prompt = refs[8]
    outs = refs[9:13]
    q2, acc, tot = refs[13:]
    for head in range(2):
        q2[head * 512 : head * 512 + 384] = q_a[head]
        q2[head * 512 + 384 : head * 512 + 512] = q_c[head]
    acc[...] = jnp.zeros_like(acc)
    tot[...] = jnp.zeros_like(tot)
    c = core[0]

    def block(ref, row, column, diagonal):
        flags = [tab[i, column] for i in range(PLANES)]

        @pl.when(flags[0] + flags[1] + flags[2] + flags[3] > 0)
        def _():
            k = ref[row : row + BLK, :HD]
            v = ref[row : row + BLK, HD:]
            scores = lax.dot_general(
                q2[...], k, (((1,), (1,)), ((), ())), preferred_element_type=jnp.float32
            )
            weights = jnp.exp2(jnp.tanh(scores * (QUERY_SCALE / SOFT_CAP)) * (SOFT_CAP * math.log2(math.e)))
            parts = []
            for i in range(2 * PLANES):
                part = weights[i * BLK : (i + 1) * BLK]
                if i % PLANES == diagonal:
                    rows_id = lax.broadcasted_iota(jnp.int32, (BLK, BLK), 0)
                    cols_id = lax.broadcasted_iota(jnp.int32, (BLK, BLK), 1)
                    flip = c * SLOTS
                    part = jnp.where((cols_id ^ flip) <= (rows_id ^ flip), part, 0.0)
                parts.append(part * flags[i % PLANES].astype(jnp.float32))
            weights = jnp.concatenate(parts, axis=0)
            tot[...] += weights
            acc[...] += jnp.dot(weights.astype(jnp.bfloat16), v, preferred_element_type=jnp.float32)

    for source in range(4):
        for b in range(PLANES):
            ref, row = (kvs[2 * source], b * BLK) if b < 3 else (kvs[2 * source + 1], 0)
            block(ref, row, source * PLANES + b, b if source == 0 else -1)
    for b in range(PLANES):
        block(prompt, b * BLK, 4 * PLANES + b, -1)
    for head in range(2):
        for i in range(PLANES):
            lo = head * 512 + i * BLK
            total = jnp.sum(tot[lo : lo + BLK], axis=1, keepdims=True)
            outs[i][:, head * HD : (head + 1) * HD] = (acc[lo : lo + BLK] / total).astype(jnp.bfloat16)


def attend(tab, core, q_a, q_c, kvs, prompt):
    smem = pl.BlockSpec(memory_space=pltpu.SMEM)
    vmem = pl.BlockSpec(memory_space=pltpu.VMEM)
    return pl.pallas_call(
        attend_kernel,
        in_specs=[smem, smem] + [vmem] * 11,
        out_specs=[vmem] * 4,
        out_shape=[jax.ShapeDtypeStruct((BLK, 2 * HD), jnp.bfloat16)] * 4,
        scratch_shapes=[
            pltpu.VMEM((1024, HD), jnp.bfloat16),
            pltpu.VMEM((1024, HD), jnp.float32),
            pltpu.VMEM((1024, HD), jnp.float32),
        ],
        compiler_params=pltpu.CompilerParams(vmem_limit_bytes=VMEM_BYTES),
        name="attend",
    )(tab, core, q_a, q_c, *kvs, prompt)


def out_kernel(a0, a1, a2, a3, w0, wg, mine, other):
    total = jnp.dot(a0[...], w0[...], preferred_element_type=jnp.float32)
    for i, a in enumerate((a1, a2, a3)):
        w = wg[:, i].reshape(2 * HD, w0.shape[1])
        total += jnp.dot(a[...], w, preferred_element_type=jnp.float32)
    mine[...] = total[:SLOTS]
    other[...] = total[SLOTS:].astype(jnp.bfloat16)


def project_out(parts, w_own, w_far):
    tile = 512
    return pl.pallas_call(
        out_kernel,
        grid=(D // tile,),
        in_specs=[pl.BlockSpec((BLK, 2 * HD), lambda n: (0, 0))] * 4
        + [
            pl.BlockSpec((2 * HD, tile), lambda n: (0, n)),
            pl.BlockSpec((RING, 3, 2 * HD // RING, tile), lambda n: (0, 0, 0, n)),
        ],
        out_specs=[pl.BlockSpec((SLOTS, tile), lambda n: (0, n))] * 2,
        out_shape=[
            jax.ShapeDtypeStruct((SLOTS, D), jnp.float32),
            jax.ShapeDtypeStruct((SLOTS, D), jnp.bfloat16),
        ],
        compiler_params=pltpu.CompilerParams(vmem_limit_bytes=VMEM_BYTES),
        name="project_out",
    )(*parts, w_own, w_far)


def body(
    rollout_rows, pack_dest, lengths, pattern, norm_gain, w_query, w_key, w_value, w_out, post_gain
):
    bf16 = jnp.bfloat16
    n_dp = lax.axis_size("dp")
    d = lax.axis_index("dp")
    t = lax.axis_index("tensor")
    plane = t // 2
    core = t % 2
    per_peer = SLOTS // n_dp
    order_ids = jnp.arange(SLOTS, dtype=jnp.int32)

    target_dev = pack_dest // SHARD
    target_slot = pack_dest % SLOTS
    before = (target_dev[:, None] == target_dev[None, :]) & (order_ids[None, :] < order_ids[:, None])
    send_pos = target_dev * per_peer + jnp.sum(before.astype(jnp.int32), axis=1)
    placer = order_ids[:, None] == send_pos[None, :]
    send_rows = jnp.dot(placer.astype(bf16), rollout_rows, preferred_element_type=jnp.float32).astype(bf16)
    send_slots = jnp.sum(jnp.where(placer, target_slot[None, :], 0), axis=1)
    send = jnp.concatenate(
        [send_rows, jnp.broadcast_to(send_slots.astype(bf16)[:, None], (SLOTS, HD))], axis=1
    )
    width = D + HD
    got = lax.all_to_all(send.reshape(n_dp, per_peer, width), "dp", 0, 0, tiled=True).reshape(SLOTS, width)

    xy = d % RING
    rows_each = w_out.shape[0] // RING
    piece = lax.dynamic_slice_in_dim(w_out, xy * rows_each, rows_each, 0)
    far = jnp.concatenate([to(piece, NEXT), to(piece, PREV), to(piece, FAR)], axis=0)
    groups = [list(range(g * RING, (g + 1) * RING)) for g in range(n_dp // RING)]
    w_far = lax.all_gather(far, "dp", axis=0, tiled=True, axis_index_groups=groups)
    w_far = w_far.reshape(RING, 3, rows_each, D)

    early = lax.all_to_all(
        jnp.broadcast_to(send[None, :per_peer], (8, per_peer, width)), "tensor", 0, 0, tiled=True
    )
    early_rows = early[..., :D].reshape(8 * per_peer, D)
    early_slot = early[..., D].astype(jnp.int32)
    early_pos = (jnp.arange(8, dtype=jnp.int32)[:, None] * SLOTS + early_slot).reshape(-1)
    early_norm = rms_scale(early_rows.astype(jnp.float32), norm_gain).astype(bf16)
    ecos, esin = rope_tables(early_pos, lengths)
    early_k = jnp.dot(early_norm, w_key, preferred_element_type=jnp.float32)
    early_k = early_k * ecos + jnp.roll(early_k, HD // 2, axis=1) * esin
    early_v = jnp.dot(early_norm, w_value, preferred_element_type=jnp.float32)
    early_kv = jnp.concatenate([early_k, early_v], axis=1).astype(bf16)
    prompt = lax.all_to_all(
        jnp.broadcast_to(early_kv[None], (n_dp,) + early_kv.shape), "dp", 0, 0, tiled=True
    )
    prompt = prompt.reshape(n_dp, 8, per_peer, 2 * HD).transpose(1, 0, 2, 3).reshape(SHARD, 2 * HD)

    order = jnp.stack([plane, plane + 3, plane + 1, plane + 2]) % PLANES
    local = jnp.arange(SHARD, dtype=jnp.int32)
    row_ids = (
        d * SHARD
        + order[local // BLK] * BLK
        + ((local % BLK) ^ (core * SLOTS))
    )
    cos, sin = rope_tables(row_ids, lengths)

    arrange = order_ids[:, None] == got[:, D].astype(jnp.int32)[None, :]
    packed = jnp.dot(arrange.astype(bf16), got[:, :D], preferred_element_type=jnp.float32).astype(bf16)
    normed = rms_scale(packed.astype(jnp.float32), norm_gain).astype(bf16)

    half = SLOTS // 2
    near_p = to(normed, NEXT)
    near_n = to(normed, PREV)
    own_s = to(normed, SIB)
    near_ps = to(near_p, SIB)
    near_ns = to(near_n, SIB)
    q_a, kv_a = project(
        [normed, own_s, near_p, near_ps, near_n, near_ns], w_query, w_key, w_value, cos[:384], sin[:384]
    )
    far_top = to(near_p[:half], NEXT)
    far_bot = to(near_n[half:], PREV)
    far_own = jnp.concatenate([far_top, far_bot], axis=0)
    far_s = to(far_own, SIB)
    q_c, kv_c = project([far_own, far_s], w_query, w_key, w_value, cos[384:], sin[384:])

    kvs = [kv_a, kv_c]
    for k in (1, 2, 3):
        shift = [(s, s + k) for s in range(n_dp - k)]
        kvs += [lax.ppermute(kv_a, "dp", shift), lax.ppermute(kv_c, "dp", shift)]

    pat = pattern[order]
    columns = []
    valid = []
    for k in range(4):
        columns.append(jnp.maximum(d - k, 0) * PLANES + order)
        valid.append(jnp.broadcast_to((d - k >= 1) | (k == 0), (PLANES,)))
    columns.append(jnp.arange(PLANES, dtype=jnp.int32))
    valid.append(jnp.broadcast_to(d >= 1, (PLANES,)))
    tab = (pat[:, jnp.concatenate(columns)] == 1) & jnp.concatenate(valid)[None, :]
    parts = attend(tab.astype(jnp.int32), core.reshape(1).astype(jnp.int32), q_a, q_c, kvs, prompt)

    mine, other = project_out(
        [parts[0], to(parts[2], NEXT), to(parts[1], PREV), to(parts[3], FAR)], w_out, w_far
    )
    summed = mine + to(other, SIB).astype(jnp.float32)
    result = packed.astype(jnp.float32) + rms_scale(summed, post_gain)
    return result.astype(bf16)


def solution(mesh):
    placed = (
        P(("dp", "tensor"), None),
        P(("dp", "tensor")),
        P(),
        P("dp", None),
        P(),
        P(None, "tensor"),
        P(None, "tensor"),
        P(None, "tensor"),
        P("tensor", None),
        P(),
    )
    return jax.shard_map(
        body, mesh=mesh, in_specs=placed, out_specs=P(("dp", "tensor"), None), check_vma=False
    )
```

time: 570 us -> 220 us (0.39)
  waiting for transfers between devices: 293 us -> 74.9 us
  loops' own time: 89.4 us -> 0 us
  other arithmetic: 96.1 us -> 12.9 us
  starting transfers between devices: 14.8 us -> 65.9 us
  Pallas kernels: 0 us -> 34.3 us
  local copies, waits for them, and re-layouts: 37.6 us -> 12.8 us
  matrix products: 21.2 us -> 1.34 us
    all_gather x2 -> x1, waiting for transfers between devices: 207 us -> 0.01 us  [body(): lax.all_gather(far, 'dp', axis=0, tiled=True, axis_index_groups=groups)]
    another operation x129 -> x0, loops' own time: 89.4 us -> none  [the longest x1 87.4 us: attend(): return lax.fori_loop(0, block_count, step, running)]
    reduce_or x128 -> x0, other arithmetic: 82.1 us -> none  [step(): jnp.any(column == 1)]
    reduce_scatter x1 -> x0, waiting for transfers between devices: 74.8 us -> none  [body(): lax.psum_scatter(jnp.dot(heads_out, w_out, preferred_element_type=jnp.flo...]
    ppermute x0 -> x21, waiting for transfers between devices: none -> 63.6 us  [the longest x15 58.8 us: to(): return lax.ppermute(values, 'tensor', pairs)]
    ppermute x0 -> x21, starting transfers between devices: none -> 46.7 us  [the longest x15 25.5 us: to(): return lax.ppermute(values, 'tensor', pairs)]
    pallas_call x0 -> x4, Pallas kernels: none -> 34.3 us  [the longest x2 18 us: project(): pl.pallas_call(functools.partial(qkv_kernel, len(pieces)), grid=(D // til...]
    unnamed x23 -> x47, local copies, waits for them, and re-layouts: 24.7 us -> 2.22 us
  transfers between devices with their start and end apart: 5 -> 25, of which waited for: 5 -> 11; matrix products, arithmetic and copies ran while one was open for 3% -> 10% of each run, Pallas kernels for 0% -> 12%
where the time goes in v1:
time: 220 us; the launch traced here: 216 us
  waiting for transfers between devices  74.9 us (34%)
  starting transfers between devices  65.9 us (30%)
  Pallas kernels  34.3 us (16%)
  between operations  14 us (6%)
  other arithmetic  12.9 us (6%)
  local copies, waits for them, and re-layouts  12.8 us (6%)
    ppermute x15, waiting for transfers between devices, to(): return lax.ppermute(values, 'tensor', pairs)  58.8 us
    ppermute x15, starting transfers between devices, to(): return lax.ppermute(values, 'tensor', pairs)  25.5 us
    ppermute x6, starting transfers between devices, body(): kvs += [lax.ppermute(kv_a, 'dp', shift), lax.ppermute(kv_c, 'dp', shift)]  21.2 us
    pallas_call x2, Pallas kernels, project(): pl.pallas_call(functools.partial(qkv_kernel, len(pieces)), grid=(D // til...  18 us
    all_to_all x1, waiting for transfers between devices, body(): lax.all_to_all(send.reshape(n_dp, per_peer, width), 'dp', 0, 0, tiled=True)  8.85 us
    pallas_call x1, Pallas kernels, project_out(): pl.pallas_call(out_kernel, grid=(D // tile,), in_specs=[pl.BlockSpec((BLK...  8.8 us
    all_to_all x1, starting transfers between devices, body(): lax.all_to_all(send.reshape(n_dp, per_peer, width), 'dp', 0, 0, tiled=True)  8.46 us
    pallas_call x1, Pallas kernels, attend(): pl.pallas_call(attend_kernel, in_specs=[smem, smem] + [vmem] * 11, out_sp...  7.52 us
  transfers between devices with their start and end apart: 25, of which 11 were waited for; matrix products, arithmetic and copies ran while one was open for 10% of the time, Pallas kernels for 12%

profile of v1, /device:TPU:40, one launch (start us, length us, event | category | flops | bytes accessed | tf_op | source)
XLA Modules:
  0.0 216.0 jit_solution(2912068511645637024)
XLA Ops:
  6.5 1.0 constant_dynamic-slice_fusion
  7.5 3.3 %collective-permute-start.17 = (bf16[16,4608]{1,0:T(8,128)(2,1)S(1)}, bf16[16,4608]{1,0:T(8,128)(2,1)S(1)}, u32[]{:S(2)}, u32[]{:S(2)}) collective-permute-start(bf16[16,4608]{1,0:T(8,128)(2,1)S(1)} %constant_dynamic-slice_fusion), channel_id=1, source_target_pairs={{0,2},{1,3},{2,4},{3,5},{4,6},{5,7},{6,0},{7,1},{8,10},{9,11},{10,... | collective-permute-start | bytes 442376 | tf_op jit(solution)/shard_map/ppermute | solution.py:54
  10.9 2.2 %collective-permute-start.18 = (bf16[16,4608]{1,0:T(8,128)(2,1)S(1)}, bf16[16,4608]{1,0:T(8,128)(2,1)S(1)}, u32[]{:S(2)}, u32[]{:S(2)}) collective-permute-start(bf16[16,4608]{1,0:T(8,128)(2,1)S(1)} %constant_dynamic-slice_fusion), channel_id=1, source_target_pairs={{0,6},{1,7},{2,0},{3,1},{4,2},{5,3},{6,4},{7,5},{8,14},{9,15},{10,... | collective-permute-start | bytes 442376 | tf_op jit(solution)/shard_map/ppermute | solution.py:54
  13.1 4.9 %collective-permute-start.19 = (bf16[16,4608]{1,0:T(8,128)(2,1)S(1)}, bf16[16,4608]{1,0:T(8,128)(2,1)S(1)}, u32[]{:S(2)}, u32[]{:S(2)}) collective-permute-start(bf16[16,4608]{1,0:T(8,128)(2,1)S(1)} %constant_dynamic-slice_fusion), channel_id=1, source_target_pairs={{0,4},{1,5},{2,6},{3,7},{4,0},{5,1},{6,2},{7,3},{8,12},{9,13},{10,... | collective-permute-start | bytes 442376 | tf_op jit(solution)/shard_map/ppermute | solution.py:54
  18.0 3.1 %collective-permute-done.17 = bf16[16,4608]{1,0:T(8,128)(2,1)S(1)} collective-permute-done((bf16[16,4608]{1,0:T(8,128)(2,1)S(1)}, bf16[16,4608]{1,0:T(8,128)(2,1)S(1)}, u32[]{:S(2)}, u32[]{:S(2)}) %collective-permute-start.17) | collective-permute-done | bytes 147488 | tf_op jit(solution)/shard_map/ppermute | solution.py:54
  21.2 9.1 %collective-permute-done.19 = bf16[16,4608]{1,0:T(8,128)(2,1)S(1)} collective-permute-done((bf16[16,4608]{1,0:T(8,128)(2,1)S(1)}, bf16[16,4608]{1,0:T(8,128)(2,1)S(1)}, u32[]{:S(2)}, u32[]{:S(2)}) %collective-permute-start.19) | collective-permute-done | bytes 147488 | tf_op jit(solution)/shard_map/ppermute | solution.py:54
  30.3 0.8 pad_maximum_fusion.1
  31.4 0.3 convolution_convert_fusion.1
  31.8 0.7 broadcast_in_dim.33
  32.6 3.4 %all-to-all-start.1 = ((bf16[8,2,4736]{2,1,0:T(2,128)(2,1)}), bf16[8,2,4736]{2,1,0:T(2,128)(2,1)S(1)}, u32[]{:S(2)}, u32[]{:S(2)}) async-start(bf16[8,2,4736]{2,1,0:T(2,128)(2,1)} %broadcast_in_dim.33), calls=%async_computation.1 | async-start | bytes 303104 | tf_op jit(solution)/shard_map/all_to_all | solution.py:238
  36.4 0.6 fusion.27
  37.0 2.4 %fusion.15 = s32[512,1]{0,1:T(1,128)S(1)} fusion(s32[]{:T(128)S(6)} %mul.173, s32[]{:T(128)} %bitcast.16, s32[]{:T(128)} %bitcast.17, s32[]{:T(128)} %bitcast.19, s32[]{:T(128)} %bitcast.18), kind=kLoop, calls=%fused_computation.76 | loop fusion | flops 9728 | bytes 2068 | tf_op jit(solution)/shard_map/add | solution.py:258
  39.6 1.0 multiply_sine_fusion
  40.6 1.0 fusion.2
  41.6 1.0 reshape.905
  42.9 2.5 %all-to-all-done.1 = bf16[8,2,4736]{2,1,0:T(2,128)(2,1)S(1)} async-done(((bf16[8,2,4736]{2,1,0:T(2,128)(2,1)}), bf16[8,2,4736]{2,1,0:T(2,128)(2,1)S(1)}, u32[]{:S(2)}, u32[]{:S(2)}) %all-to-all-start.1) | async-done | bytes 151584 | tf_op jit(solution)/shard_map/all_to_all | solution.py:238
  45.4 8.5 %all-to-all-start = ((bf16[32,2,4736]{2,1,0:T(2,128)(2,1)}), bf16[32,2,4736]{2,1,0:T(2,128)(2,1)S(1)}, u32[]{:S(2)}, u32[]{:S(2)}) async-start(bf16[32,2,4736]{2,1,0:T(2,128)(2,1)} %reshape.905), calls=%async_computation | async-start | bytes 1212416 | tf_op jit(solution)/shard_map/all_to_all | solution.py:228
  54.7 0.8 slice_convert_fusion
  55.5 8.8 %all-to-all-done = bf16[32,2,4736]{2,1,0:T(2,128)(2,1)S(1)} async-done(((bf16[32,2,4736]{2,1,0:T(2,128)(2,1)}), bf16[32,2,4736]{2,1,0:T(2,128)(2,1)S(1)}, u32[]{:S(2)}, u32[]{:S(2)}) %all-to-all-start) | async-done | bytes 606240 | tf_op jit(solution)/shard_map/all_to_all | solution.py:228
  64.7 0.4 multiply_reduce_fusion.1
  65.3 1.0 multiply_convert_fusion.refs_0_
  66.3 1.4 collective-permute-start.1
  67.7 1.2 reshape.914
  69.0 0.3 fusion.25
  69.3 2.8 %collective-permute-start.3 = (bf16[64,4608]{1,0:T(8,128)(2,1)}, bf16[64,4608]{1,0:T(8,128)(2,1)S(1)}, u32[]{:S(2)}, u32[]{:S(2)}) collective-permute-start(bf16[64,4608]{1,0:T(8,128)(2,1)} %multiply_convert_fusion.refs_0_), channel_id=1, source_target_pairs={{0,6},{1,7},{2,0},{3,1},{4,2},{5,3},{6,4},{7,5},{8,14},{9,15},{10,... | collective-permute-start | bytes 1769480 | tf_op jit(solution)/shard_map/ppermute | solution.py:54
  72.2 24.1 %collective-permute-done.1.refs_2_ = bf16[64,4608]{1,0:T(8,128)(2,1)} collective-permute-done((bf16[64,4608]{1,0:T(8,128)(2,1)}, bf16[64,4608]{1,0:T(8,128)(2,1)}, u32[]{:S(2)}, u32[]{:S(2)}) %collective-permute-start.1) | collective-permute-done | bytes 589856 | tf_op jit(solution)/shard_map/ppermute | solution.py:54
  96.3 1.0 slice.74
  97.3 0.7 collective-permute-start.5
  98.0 0.3 convolution_convert_fusion.2
  98.5 3.6 %collective-permute-start.6 = (bf16[32,4608]{1,0:T(8,128)(2,1)S(1)}, bf16[32,4608]{1,0:T(8,128)(2,1)S(1)}, u32[]{:S(2)}, u32[]{:S(2)}) collective-permute-start(bf16[32,4608]{1,0:T(8,128)(2,1)S(1)} %slice.75), channel_id=1, source_target_pairs={{0,6},{1,7},{2,0},{3,1},{4,2},{5,3},{6,4},{7,5},{8,14},{9,15},{10,... | collective-permute-start | bytes 884744 | tf_op jit(solution)/shard_map/ppermute | solution.py:54
  102.3 0.3 collective-permute-start.4
  102.7 5.7 %collective-permute-done.5 = bf16[32,4608]{1,0:T(8,128)(2,1)S(1)} collective-permute-done((bf16[32,4608]{1,0:T(8,128)(2,1)S(1)}, bf16[32,4608]{1,0:T(8,128)(2,1)S(1)}, u32[]{:S(2)}, u32[]{:S(2)}) %collective-permute-start.5) | collective-permute-done | bytes 294944 | tf_op jit(solution)/shard_map/ppermute | solution.py:54
  108.4 0.7 constant_dynamic-update-slice_fusion.1
  109.1 7.1 %collective-permute-done.6 = bf16[32,4608]{1,0:T(8,128)(2,1)S(1)} collective-permute-done((bf16[32,4608]{1,0:T(8,128)(2,1)S(1)}, bf16[32,4608]{1,0:T(8,128)(2,1)S(1)}, u32[]{:S(2)}, u32[]{:S(2)}) %collective-permute-start.6) | collective-permute-done | bytes 294944 | tf_op jit(solution)/shard_map/ppermute | solution.py:54
  116.2 0.7 constant_dynamic-update-slice_fusion.refs_0_
  117.1 0.7 broadcast_in_dim.34
  117.8 7.3 %all-to-all-start.2 = ((bf16[32,16,256]{2,1,0:T(8,128)(2,1)}), bf16[32,16,256]{2,1,0:T(8,128)(2,1)S(1)}, u32[]{:S(2)}, u32[]{:S(2)}) async-start(bf16[32,16,256]{2,1,0:T(8,128)(2,1)} %broadcast_in_dim.34), calls=%async_computation.2 | async-start | bytes 524288 | tf_op jit(solution)/shard_map/all_to_all | solution.py:250
  125.3 10.1 %project.2 = (bf16[2,384,128]{2,1,0:T(8,128)(2,1)}, bf16[384,256]{1,0:T(8,128)(2,1)}) custom-call(bf16[64,4608]{1,0:T(8,128)(2,1)} %multiply_convert_fusion.refs_0_, bf16[64,4608]{1,0:T(8,128)(2,1)} %collective-permute-done.refs_1_, bf16[64,4608]{1,0:T(8,128)(2,1)} %collective-permute-done.1.refs_2_, bf16[64,4608]{1,0:T(8,128)(2,1)} %collective-permute-done.2.refs_3_, ...), custom_call_target="tpu_custom_call" | custom-call | tf_op jit(solution)/shard_map/project/pallas_call | solution.py:91
  135.5 4.9 %collective-permute-start.10 = (bf16[384,256]{1,0:T(8,128)(2,1)}, bf16[384,256]{1,0:T(8,128)(2,1)S(1)}, u32[]{:S(2)}, u32[]{:S(2)}) collective-permute-start(bf16[384,256]{1,0:T(8,128)(2,1)} %get-tuple-element.17.refs_0_), channel_id=1, source_target_pairs={{0,16},{8,24},{16,32},{24,40},{32,48},{40,56},{48,64},{56,72},{64,... | collective-permute-start | bytes 589832 | tf_op jit(solution)/shard_map/ppermute | solution.py:286
  140.4 0.6 gather_fusion
  141.1 0.6 gather_fusion.1
  141.9 0.7 pad_maximum_fusion.2
  142.6 4.0 %collective-permute-start.12 = (bf16[384,256]{1,0:T(8,128)(2,1)}, bf16[384,256]{1,0:T(8,128)(2,1)S(1)}, u32[]{:S(2)}, u32[]{:S(2)}) collective-permute-start(bf16[384,256]{1,0:T(8,128)(2,1)} %get-tuple-element.17.refs_0_), channel_id=1, source_target_pairs={{0,24},{8,32},{16,40},{24,48},{32,56},{40,64},{48,72},{56,80},{64,... | collective-permute-start | bytes 589832 | tf_op jit(solution)/shard_map/ppermute | solution.py:286
  146.6 2.8 %collective-permute-start.8 = (bf16[384,256]{1,0:T(8,128)(2,1)}, bf16[384,256]{1,0:T(8,128)(2,1)S(1)}, u32[]{:S(2)}, u32[]{:S(2)}) collective-permute-start(bf16[384,256]{1,0:T(8,128)(2,1)} %get-tuple-element.17.refs_0_), channel_id=1, source_target_pairs={{0,8},{8,16},{16,24},{24,32},{32,40},{40,48},{48,56},{56,64},{64,7... | collective-permute-start | bytes 589832 | tf_op jit(solution)/shard_map/ppermute | solution.py:286
  149.4 7.8 %project.3 = (bf16[2,128,128]{2,1,0:T(8,128)(2,1)}, bf16[128,256]{1,0:T(8,128)(2,1)}) custom-call(bf16[64,4608]{1,0:T(8,128)(2,1)} %constant_dynamic-update-slice_fusion.refs_0_, bf16[64,4608]{1,0:T(8,128)(2,1)} %collective-permute-done.7.refs_1_, bf16[4608,256]{1,0:T(8,128)(2,1)} %refs_2_.1, bf16[4608,128]{1,0:T(8,128)(2,1)} %refs_3_.1, ...), custom_call_target="tpu_custom_call" | custom-call | tf_op jit(solution)/shard_map/project/pallas_call | solution.py:91
  157.2 3.1 %collective-permute-start.11 = (bf16[128,256]{1,0:T(8,128)(2,1)}, bf16[128,256]{1,0:T(8,128)(2,1)S(1)}, u32[]{:S(2)}, u32[]{:S(2)}) collective-permute-start(bf16[128,256]{1,0:T(8,128)(2,1)} %get-tuple-element.18.refs_1_), channel_id=1, source_target_pairs={{0,16},{8,24},{16,32},{24,40},{32,48},{40,56},{48,64},{56,72},{64,... | collective-permute-start | bytes 196616 | tf_op jit(solution)/shard_map/ppermute | solution.py:286
  160.3 4.6 %collective-permute-start.13 = (bf16[128,256]{1,0:T(8,128)(2,1)}, bf16[128,256]{1,0:T(8,128)(2,1)S(1)}, u32[]{:S(2)}, u32[]{:S(2)}) collective-permute-start(bf16[128,256]{1,0:T(8,128)(2,1)} %get-tuple-element.18.refs_1_), channel_id=1, source_target_pairs={{0,24},{8,32},{16,40},{24,48},{32,56},{40,64},{48,72},{56,80},{64,... | collective-permute-start | bytes 196616 | tf_op jit(solution)/shard_map/ppermute | solution.py:286
  164.9 1.9 collective-permute-start.9
  166.9 0.6 convert_bitcast_fusion.tab
  167.6 0.3 copy.37
  167.8 0.8 reshape.911.refs_8_
  168.7 4.7 %collective-permute-done.9.refs_3_ = bf16[128,256]{1,0:T(8,128)(2,1)S(1)} collective-permute-done((bf16[128,256]{1,0:T(8,128)(2,1)}, bf16[128,256]{1,0:T(8,128)(2,1)S(1)}, u32[]{:S(2)}, u32[]{:S(2)}) %collective-permute-start.9) | collective-permute-done | bytes 65568 | tf_op jit(solution)/shard_map/ppermute | solution.py:286
  173.5 0.6 copy-done.19
  174.0 7.5 %attend.1 = (bf16[128,256]{1,0:T(8,128)(2,1)}, bf16[128,256]{1,0:T(8,128)(2,1)}, bf16[128,256]{1,0:T(8,128)(2,1)}, bf16[128,256]{1,0:T(8,128)(2,1)}) custom-call(s32[4,20]{1,0:T(4,128)} %convert_bitcast_fusion.tab, s32[1]{0:T(128)} %bitcast.15.core, bf16[2,384,128]{2,1,0:T(8,128)(2,1)} %get-tuple-element.15.q_a, bf16[2,128,128]{2,1,0:T(8,128)(2,1)} %get-tuple-element.16.q_c, ...), custom_call_target="tpu_custom_call" | custom-call | tf_op jit(solution)/shard_map/attend/pallas_call | solution.py:161
  181.6 2.1 collective-permute-start.14
  183.6 2.1 collective-permute-start.15
  185.7 1.6 collective-permute-start.16
  187.3 1.9 collective-permute-done.14.a1
  189.2 5.6 %collective-permute-done.16.a3 = bf16[128,256]{1,0:T(8,128)(2,1)S(1)} collective-permute-done((bf16[128,256]{1,0:T(8,128)(2,1)}, bf16[128,256]{1,0:T(8,128)(2,1)S(1)}, u32[]{:S(2)}, u32[]{:S(2)}) %collective-permute-start.16) | collective-permute-done | bytes 65568 | tf_op jit(solution)/shard_map/ppermute | solution.py:54
  194.8 0.6 copy-done.16
  195.4 8.8 %project_out.1 = (f32[64,4608]{1,0:T(8,128)}, bf16[64,4608]{1,0:T(8,128)(2,1)}) custom-call(bf16[128,256]{1,0:T(8,128)(2,1)} %get-tuple-element.19.a0, bf16[128,256]{1,0:T(8,128)(2,1)} %copy-done.14, bf16[128,256]{1,0:T(8,128)(2,1)} %copy-done.15, bf16[128,256]{1,0:T(8,128)(2,1)} %copy-done.16, bf16[256,4608]{1,0:T(8,128)(2,1)} %w0.1, ...), custom_call_target="tpu_custom_call" | custom-call | tf_op jit(solution)/shard_map/project_out/pallas_call | solution.py:187
  204.3 2.2 %collective-permute-done.20 = bf16[64,4608]{1,0:T(8,128)(2,1)S(1)} collective-permute-done((bf16[64,4608]{1,0:T(8,128)(2,1)}, bf16[64,4608]{1,0:T(8,128)(2,1)S(1)}, u32[]{:S(2)}, u32[]{:S(2)}) %collective-permute-start.20) | collective-permute-done | bytes 589856 | tf_op jit(solution)/shard_map/ppermute | solution.py:54
  206.5 1.5 multiply_reduce_fusion
  208.1 1.1 add_convert_fusion
  (115 shorter events, 4.0 us)
Async XLA Ops:
  6.5 24.9 %copy-start = (bf16[64,4608]{1,0:T(8,128)(2,1)S(1)}, bf16[64,4608]{1,0:T(8,128)(2,1)}, u32[]{:S(2)}) copy-start(bf16[64,4608]{1,0:T(8,128)(2,1)} %param.10) | copy-start | bytes 1769476
  6.5 24.5 %copy-start.22 = (s32[64]{0:T(128)S(1)}, s32[64]{0:T(128)}, u32[]{:S(2)}) copy-start(s32[64]{0:T(128)} %param.11) | copy-start | bytes 772
  6.5 188.2 %all-gather.2.cloned.1.call-start = ((), (), s32[]{:S(2)}) async-start(), calls=%async_computation.3 | async-start | bytes 7520256 | tf_op jit(solution)/shard_map/all_gather | solution.py:235
  7.5 13.6 %collective-permute-start.17 = (bf16[16,4608]{1,0:T(8,128)(2,1)S(1)}, bf16[16,4608]{1,0:T(8,128)(2,1)S(1)}, u32[]{:S(2)}, u32[]{:S(2)}) collective-permute-start(bf16[16,4608]{1,0:T(8,128)(2,1)S(1)} %constant_dynamic-slice_fusion), channel_id=1, source_target_pairs={{0,2},{1,3},{2,4},{3,5},{4,6},{5,7},{6,0},{7,1},{8,10},{9,11},{10,... | collective-permute-start | bytes 442376 | tf_op jit(solution)/shard_map/ppermute | solution.py:54
  10.9 10.3 %collective-permute-start.18 = (bf16[16,4608]{1,0:T(8,128)(2,1)S(1)}, bf16[16,4608]{1,0:T(8,128)(2,1)S(1)}, u32[]{:S(2)}, u32[]{:S(2)}) collective-permute-start(bf16[16,4608]{1,0:T(8,128)(2,1)S(1)} %constant_dynamic-slice_fusion), channel_id=1, source_target_pairs={{0,6},{1,7},{2,0},{3,1},{4,2},{5,3},{6,4},{7,5},{8,14},{9,15},{10,... | collective-permute-start | bytes 442376 | tf_op jit(solution)/shard_map/ppermute | solution.py:54
  13.1 17.1 %collective-permute-start.19 = (bf16[16,4608]{1,0:T(8,128)(2,1)S(1)}, bf16[16,4608]{1,0:T(8,128)(2,1)S(1)}, u32[]{:S(2)}, u32[]{:S(2)}) collective-permute-start(bf16[16,4608]{1,0:T(8,128)(2,1)S(1)} %constant_dynamic-slice_fusion), channel_id=1, source_target_pairs={{0,4},{1,5},{2,6},{3,7},{4,0},{5,1},{6,2},{7,3},{8,12},{9,13},{10,... | collective-permute-start | bytes 442376 | tf_op jit(solution)/shard_map/ppermute | solution.py:54
  31.3 4.7 %copy-start.21 = (s32[17]{0:T(128)S(1)}, s32[17]{0:T(128)}, u32[]{:S(2)}) copy-start(s32[17]{0:T(128)} %param.12) | copy-start | bytes 208
  32.6 12.9 %all-to-all-start.1 = ((bf16[8,2,4736]{2,1,0:T(2,128)(2,1)}), bf16[8,2,4736]{2,1,0:T(2,128)(2,1)S(1)}, u32[]{:S(2)}, u32[]{:S(2)}) async-start(bf16[8,2,4736]{2,1,0:T(2,128)(2,1)} %broadcast_in_dim.33), calls=%async_computation.1 | async-start | bytes 303104 | tf_op jit(solution)/shard_map/all_to_all | solution.py:238
  40.6 1.0 copy-start.4
  40.6 1.0 copy-start.6
  45.4 18.9 %all-to-all-start = ((bf16[32,2,4736]{2,1,0:T(2,128)(2,1)}), bf16[32,2,4736]{2,1,0:T(2,128)(2,1)S(1)}, u32[]{:S(2)}, u32[]{:S(2)}) async-start(bf16[32,2,4736]{2,1,0:T(2,128)(2,1)} %reshape.905), calls=%async_computation | async-start | bytes 1212416 | tf_op jit(solution)/shard_map/all_to_all | solution.py:228
  64.6 0.7 copy-start.12
  65.3 3.6 %copy-start.1 = (bf16[4608,128]{1,0:T(8,128)(2,1)S(1)}, bf16[4608,128]{1,0:T(8,128)(2,1)}, u32[]{:S(2)}) copy-start(bf16[4608,128]{1,0:T(8,128)(2,1)} %refs_3_.1) | copy-start | bytes 3538948
  66.3 30.0 %collective-permute-start.1 = (bf16[64,4608]{1,0:T(8,128)(2,1)}, bf16[64,4608]{1,0:T(8,128)(2,1)}, u32[]{:S(2)}, u32[]{:S(2)}) collective-permute-start(bf16[64,4608]{1,0:T(8,128)(2,1)} %multiply_convert_fusion.refs_0_), channel_id=1, source_target_pairs={{0,2},{1,3},{2,4},{3,5},{4,6},{5,7},{6,0},{7,1},{8,10},{9,11},{10,... | collective-permute-start | bytes 1769480 | tf_op jit(solution)/shard_map/ppermute | solution.py:54
  68.9 29.1 %copy-start.2 = (bf16[4608,128]{1,0:T(8,128)(2,1)S(1)}, bf16[4608,128]{1,0:T(8,128)(2,1)}, u32[]{:S(2)}) copy-start(bf16[4608,128]{1,0:T(8,128)(2,1)} %refs_4_.1) | copy-start | bytes 3538948
  69.3 29.2 %collective-permute-start.3 = (bf16[64,4608]{1,0:T(8,128)(2,1)}, bf16[64,4608]{1,0:T(8,128)(2,1)S(1)}, u32[]{:S(2)}, u32[]{:S(2)}) collective-permute-start(bf16[64,4608]{1,0:T(8,128)(2,1)} %multiply_convert_fusion.refs_0_), channel_id=1, source_target_pairs={{0,6},{1,7},{2,0},{3,1},{4,2},{5,3},{6,4},{7,5},{8,14},{9,15},{10,... | collective-permute-start | bytes 1769480 | tf_op jit(solution)/shard_map/ppermute | solution.py:54
  97.3 11.1 %collective-permute-start.5 = (bf16[32,4608]{1,0:T(8,128)(2,1)S(1)}, bf16[32,4608]{1,0:T(8,128)(2,1)S(1)}, u32[]{:S(2)}, u32[]{:S(2)}) collective-permute-start(bf16[32,4608]{1,0:T(8,128)(2,1)S(1)} %slice.74), channel_id=1, source_target_pairs={{0,2},{1,3},{2,4},{3,5},{4,6},{5,7},{6,0},{7,1},{8,10},{9,11},{10,... | collective-permute-start | bytes 884744 | tf_op jit(solution)/shard_map/ppermute | solution.py:54
  98.4 26.9 %collective-permute-start = (bf16[64,4608]{1,0:T(8,128)(2,1)}, bf16[64,4608]{1,0:T(8,128)(2,1)}, u32[]{:S(2)}, u32[]{:S(2)}) collective-permute-start(bf16[64,4608]{1,0:T(8,128)(2,1)} %multiply_convert_fusion.refs_0_), channel_id=1, source_target_pairs={{0,1},{1,0},{2,3},{3,2},{4,5},{5,4},{6,7},{7,6},{8,9},{9,8},{10,11... | collective-permute-start | bytes 1769480 | tf_op jit(solution)/shard_map/ppermute | solution.py:54
  98.5 19.4 %copy-start.8 = (bf16[64,4608]{1,0:T(8,128)(2,1)}, bf16[64,4608]{1,0:T(8,128)(2,1)S(1)}, u32[]{:S(2)}) copy-start(bf16[64,4608]{1,0:T(8,128)(2,1)S(1)} %collective-permute-done.3.refs_4_) | copy-start | bytes 1769476
  98.5 17.7 %collective-permute-start.6 = (bf16[32,4608]{1,0:T(8,128)(2,1)S(1)}, bf16[32,4608]{1,0:T(8,128)(2,1)S(1)}, u32[]{:S(2)}, u32[]{:S(2)}) collective-permute-start(bf16[32,4608]{1,0:T(8,128)(2,1)S(1)} %slice.75), channel_id=1, source_target_pairs={{0,6},{1,7},{2,0},{3,1},{4,2},{5,3},{6,4},{7,5},{8,14},{9,15},{10,... | collective-permute-start | bytes 884744 | tf_op jit(solution)/shard_map/ppermute | solution.py:54
  102.2 23.1 %collective-permute-start.2 = (bf16[64,4608]{1,0:T(8,128)(2,1)}, bf16[64,4608]{1,0:T(8,128)(2,1)}, u32[]{:S(2)}, u32[]{:S(2)}) collective-permute-start(bf16[64,4608]{1,0:T(8,128)(2,1)} %collective-permute-done.1.refs_2_), channel_id=1, source_target_pairs={{0,1},{1,0},{2,3},{3,2},{4,5},{5,4},{6,7},{7,6},{8,9},{9,8},{10,11... | collective-permute-start | bytes 1769480 | tf_op jit(solution)/shard_map/ppermute | solution.py:54
  102.3 23.0 %collective-permute-start.4 = (bf16[64,4608]{1,0:T(8,128)(2,1)S(1)}, bf16[64,4608]{1,0:T(8,128)(2,1)}, u32[]{:S(2)}, u32[]{:S(2)}) collective-permute-start(bf16[64,4608]{1,0:T(8,128)(2,1)S(1)} %collective-permute-done.3.refs_4_), channel_id=1, source_target_pairs={{0,1},{1,0},{2,3},{3,2},{4,5},{5,4},{6,7},{7,6},{8,9},{9,8},{10,11... | collective-permute-start | bytes 1769480 | tf_op jit(solution)/shard_map/ppermute | solution.py:54
  116.9 32.4 %collective-permute-start.7 = (bf16[64,4608]{1,0:T(8,128)(2,1)}, bf16[64,4608]{1,0:T(8,128)(2,1)}, u32[]{:S(2)}, u32[]{:S(2)}) collective-permute-start(bf16[64,4608]{1,0:T(8,128)(2,1)} %constant_dynamic-update-slice_fusion.refs_0_), channel_id=1, source_target_pairs={{0,1},{1,0},{2,3},{3,2},{4,5},{5,4},{6,7},{7,6},{8,9},{9,8},{10,11... | collective-permute-start | bytes 1769480 | tf_op jit(solution)/shard_map/ppermute | solution.py:54
  117.8 49.6 %all-to-all-start.2 = ((bf16[32,16,256]{2,1,0:T(8,128)(2,1)}), bf16[32,16,256]{2,1,0:T(8,128)(2,1)S(1)}, u32[]{:S(2)}, u32[]{:S(2)}) async-start(bf16[32,16,256]{2,1,0:T(8,128)(2,1)} %broadcast_in_dim.34), calls=%async_computation.2 | async-start | bytes 524288 | tf_op jit(solution)/shard_map/all_to_all | solution.py:250
  125.3 15.1 %copy-start.13 = (s32[4,128]{1,0:T(4,128)S(1)}, s32[4,128]{1,0:T(4,128)}, u32[]{:S(2)}) copy-start(s32[4,128]{1,0:T(4,128)} %param.13) | copy-start | bytes 6148
  125.3 16.5 %copy-start.5 = (f32[512,64]{1,0:T(8,128)S(1)}, f32[512,64]{1,0:T(8,128)}, u32[]{:S(2)}) copy-start(f32[512,64]{1,0:T(8,128)} %copy-done.4) | copy-start | bytes 393220
  125.3 16.5 %copy-start.7 = (f32[512,64]{1,0:T(8,128)S(1)}, f32[512,64]{1,0:T(8,128)}, u32[]{:S(2)}) copy-start(f32[512,64]{1,0:T(8,128)} %copy-done.6) | copy-start | bytes 393220
  135.5 29.5 %collective-permute-start.10 = (bf16[384,256]{1,0:T(8,128)(2,1)}, bf16[384,256]{1,0:T(8,128)(2,1)S(1)}, u32[]{:S(2)}, u32[]{:S(2)}) collective-permute-start(bf16[384,256]{1,0:T(8,128)(2,1)} %get-tuple-element.17.refs_0_), channel_id=1, source_target_pairs={{0,16},{8,24},{16,32},{24,40},{32,48},{40,56},{48,64},{56,72},{64,... | collective-permute-start | bytes 589832 | tf_op jit(solution)/shard_map/ppermute | solution.py:286
  142.6 26.0 %collective-permute-start.12 = (bf16[384,256]{1,0:T(8,128)(2,1)}, bf16[384,256]{1,0:T(8,128)(2,1)S(1)}, u32[]{:S(2)}, u32[]{:S(2)}) collective-permute-start(bf16[384,256]{1,0:T(8,128)(2,1)} %get-tuple-element.17.refs_0_), channel_id=1, source_target_pairs={{0,24},{8,32},{16,40},{24,48},{32,56},{40,64},{48,72},{56,80},{64,... | collective-permute-start | bytes 589832 | tf_op jit(solution)/shard_map/ppermute | solution.py:286
  146.6 22.1 %collective-permute-start.8 = (bf16[384,256]{1,0:T(8,128)(2,1)}, bf16[384,256]{1,0:T(8,128)(2,1)S(1)}, u32[]{:S(2)}, u32[]{:S(2)}) collective-permute-start(bf16[384,256]{1,0:T(8,128)(2,1)} %get-tuple-element.17.refs_0_), channel_id=1, source_target_pairs={{0,8},{8,16},{16,24},{24,32},{32,40},{40,48},{48,56},{56,64},{64,7... | collective-permute-start | bytes 589832 | tf_op jit(solution)/shard_map/ppermute | solution.py:286
  157.2 11.4 %collective-permute-start.11 = (bf16[128,256]{1,0:T(8,128)(2,1)}, bf16[128,256]{1,0:T(8,128)(2,1)S(1)}, u32[]{:S(2)}, u32[]{:S(2)}) collective-permute-start(bf16[128,256]{1,0:T(8,128)(2,1)} %get-tuple-element.18.refs_1_), channel_id=1, source_target_pairs={{0,16},{8,24},{16,32},{24,40},{32,48},{40,56},{48,64},{56,72},{64,... | collective-permute-start | bytes 196616 | tf_op jit(solution)/shard_map/ppermute | solution.py:286
  160.3 8.4 %collective-permute-start.13 = (bf16[128,256]{1,0:T(8,128)(2,1)}, bf16[128,256]{1,0:T(8,128)(2,1)S(1)}, u32[]{:S(2)}, u32[]{:S(2)}) collective-permute-start(bf16[128,256]{1,0:T(8,128)(2,1)} %get-tuple-element.18.refs_1_), channel_id=1, source_target_pairs={{0,24},{8,32},{16,40},{24,48},{32,56},{40,64},{48,72},{56,80},{64,... | collective-permute-start | bytes 196616 | tf_op jit(solution)/shard_map/ppermute | solution.py:286
  164.9 8.5 %copy-start.9 = (bf16[384,256]{1,0:T(8,128)(2,1)}, bf16[384,256]{1,0:T(8,128)(2,1)S(1)}, u32[]{:S(2)}) copy-start(bf16[384,256]{1,0:T(8,128)(2,1)S(1)} %collective-permute-done.10.refs_4_) | copy-start | bytes 589828
  164.9 8.5 %collective-permute-start.9 = (bf16[128,256]{1,0:T(8,128)(2,1)}, bf16[128,256]{1,0:T(8,128)(2,1)S(1)}, u32[]{:S(2)}, u32[]{:S(2)}) collective-permute-start(bf16[128,256]{1,0:T(8,128)(2,1)} %get-tuple-element.18.refs_1_), channel_id=1, source_target_pairs={{0,8},{8,16},{16,24},{24,32},{32,40},{40,48},{48,56},{56,64},{64,7... | collective-permute-start | bytes 196616 | tf_op jit(solution)/shard_map/ppermute | solution.py:286
  168.6 4.8 %copy-start.10 = (bf16[384,256]{1,0:T(8,128)(2,1)}, bf16[384,256]{1,0:T(8,128)(2,1)S(1)}, u32[]{:S(2)}) copy-start(bf16[384,256]{1,0:T(8,128)(2,1)S(1)} %collective-permute-done.12.refs_6_) | copy-start | bytes 589828
  168.7 4.8 %copy-start.11 = (bf16[384,256]{1,0:T(8,128)(2,1)}, bf16[384,256]{1,0:T(8,128)(2,1)S(1)}, u32[]{:S(2)}) copy-start(bf16[384,256]{1,0:T(8,128)(2,1)S(1)} %collective-permute-done.8.refs_2_) | copy-start | bytes 589828
  168.7 4.8 %copy-start.17 = (bf16[128,256]{1,0:T(8,128)(2,1)}, bf16[128,256]{1,0:T(8,128)(2,1)S(1)}, u32[]{:S(2)}) copy-start(bf16[128,256]{1,0:T(8,128)(2,1)S(1)} %collective-permute-done.11.refs_5_) | copy-start | bytes 196612
  168.7 4.8 %copy-start.18 = (bf16[128,256]{1,0:T(8,128)(2,1)}, bf16[128,256]{1,0:T(8,128)(2,1)S(1)}, u32[]{:S(2)}) copy-start(bf16[128,256]{1,0:T(8,128)(2,1)S(1)} %collective-permute-done.13.refs_7_) | copy-start | bytes 196612
  173.4 0.6 copy-start.19
  181.6 7.6 %collective-permute-start.14 = (bf16[128,256]{1,0:T(8,128)(2,1)}, bf16[128,256]{1,0:T(8,128)(2,1)S(1)}, u32[]{:S(2)}, u32[]{:S(2)}) collective-permute-start(bf16[128,256]{1,0:T(8,128)(2,1)} %get-tuple-element.20), channel_id=1, source_target_pairs={{0,2},{1,3},{2,4},{3,5},{4,6},{5,7},{6,0},{7,1},{8,10},{9,11},{10,... | collective-permute-start | bytes 196616 | tf_op jit(solution)/shard_map/ppermute | solution.py:54
  183.6 5.6 %collective-permute-start.15 = (bf16[128,256]{1,0:T(8,128)(2,1)}, bf16[128,256]{1,0:T(8,128)(2,1)S(1)}, u32[]{:S(2)}, u32[]{:S(2)}) collective-permute-start(bf16[128,256]{1,0:T(8,128)(2,1)} %get-tuple-element.21), channel_id=1, source_target_pairs={{0,6},{1,7},{2,0},{3,1},{4,2},{5,3},{6,4},{7,5},{8,14},{9,15},{10,... | collective-permute-start | bytes 196616 | tf_op jit(solution)/shard_map/ppermute | solution.py:54
  185.7 9.1 %collective-permute-start.16 = (bf16[128,256]{1,0:T(8,128)(2,1)}, bf16[128,256]{1,0:T(8,128)(2,1)S(1)}, u32[]{:S(2)}, u32[]{:S(2)}) collective-permute-start(bf16[128,256]{1,0:T(8,128)(2,1)} %get-tuple-element.22), channel_id=1, source_target_pairs={{0,4},{1,5},{2,6},{3,7},{4,0},{5,1},{6,2},{7,3},{8,12},{9,13},{10,... | collective-permute-start | bytes 196616 | tf_op jit(solution)/shard_map/ppermute | solution.py:54
  189.2 5.6 %copy-start.14 = (bf16[128,256]{1,0:T(8,128)(2,1)}, bf16[128,256]{1,0:T(8,128)(2,1)S(1)}, u32[]{:S(2)}) copy-start(bf16[128,256]{1,0:T(8,128)(2,1)S(1)} %collective-permute-done.14.a1) | copy-start | bytes 196612
  189.2 5.6 %copy-start.15 = (bf16[128,256]{1,0:T(8,128)(2,1)}, bf16[128,256]{1,0:T(8,128)(2,1)S(1)}, u32[]{:S(2)}) copy-start(bf16[128,256]{1,0:T(8,128)(2,1)S(1)} %collective-permute-done.15.a2) | copy-start | bytes 196612
  194.8 0.6 copy-start.16
  204.2 3.9 %copy-start.3 = (f32[64,4608]{1,0:T(8,128)S(1)}, f32[64,4608]{1,0:T(8,128)}, u32[]{:S(2)}) copy-start(f32[64,4608]{1,0:T(8,128)} %get-tuple-element.23) | copy-start | bytes 3538948
  204.2 3.9 %copy-start.20 = (f32[4608]{0:T(1024)S(1)}, f32[4608]{0:T(1024)}, u32[]{:S(2)}) copy-start(f32[4608]{0:T(1024)} %param.19) | copy-start | bytes 55300
  204.2 2.3 %collective-permute-start.20 = (bf16[64,4608]{1,0:T(8,128)(2,1)}, bf16[64,4608]{1,0:T(8,128)(2,1)S(1)}, u32[]{:S(2)}, u32[]{:S(2)}) collective-permute-start(bf16[64,4608]{1,0:T(8,128)(2,1)} %get-tuple-element.24), channel_id=1, source_target_pairs={{0,1},{1,0},{2,3},{3,2},{4,5},{5,4},{6,7},{7,6},{8,9},{9,8},{10,11... | collective-permute-start | bytes 1769480 | tf_op jit(solution)/shard_map/ppermute | solution.py:54
Sparse Core Ops, SparseCore 0:
  31.2 73.5 all-gather.1
